TPU v7x, 512 devices: a whole 4x8x8 slice. The times are simulated.
512 devices in a mesh: ta: 64 (over z, x, core), pa: 8 (over y).
Axes of the slice: x: 4, y: 8, z: 8, core: 2. Of those that a mesh axis runs over, the one named last changes fastest.
Arguments:
- occupied_orbitals: bfloat16 [4096, 512], P('pa'), may hold values from -3 to 3
- virtual_orbitals: bfloat16 [4096, 1536], P('pa'), may hold values from -2.5 to 2.5
- occupied_gaps: float32 [512], replicated, may hold values from 0.05 to 2
- virtual_gaps: float32 [1536], replicated, may hold values from 0.05 to 2
- tile_columns: int32 [32, 8], replicated, may hold values from 0 to 31, as said below
- probe_vectors: bfloat16 [32, 4096], P(None, 'ta'), may hold values from -0.1875 to 0.1875
Outputs:
- response: float32 [64, 32, 4096], P('ta', None, 'pa')
Inputs may be any that keep to these rules, and one draw needn't show every extreme that they name: `tile_columns`: each row block lists 8 different column blocks, and every column block is listed by some row block.
All inputs are finite; a program needn't handle non-finite values.
Results may differ from a plain program's by a relative error of at most 0.00083.
Values may be sent and summed in bfloat16 or wider, within the bound.
A program may use at most 64 MiB of HBM per device.

v0:
```python
import jax
import jax.numpy as jnp
from jax import lax
from jax.sharding import PartitionSpec as P

BLK = 128
NT = 32
NVEC = 32
F_DEV = 1


def spread(value, axis, source):
    kept = jnp.where(lax.axis_index(axis) == source, value, 0).astype(value.dtype)
    return lax.psum(kept, axis)


def quadrature_grids(count_times, count_freqs):
    low_time = jnp.log(jnp.float32(0.05))
    high_time = jnp.log(jnp.float32(8.0))
    time_place = (jnp.arange(count_times, dtype=jnp.float32) + 0.5) / count_times
    times_grid = jnp.exp(low_time + (high_time - low_time) * time_place)
    weights_grid = times_grid * (high_time - low_time) / count_times
    low_freq = jnp.log(jnp.float32(0.05))
    high_freq = jnp.log(jnp.float32(20.0))
    freq_place = (jnp.arange(count_freqs, dtype=jnp.float32) + 0.5) / count_freqs
    freqs_grid = jnp.exp(low_freq + (high_freq - low_freq) * freq_place)
    cosine_table = 2.0 * weights_grid[None, :] * jnp.cos(freqs_grid[:, None] * times_grid[None, :])
    return (times_grid, cosine_table)


def shards(
    occupied_orbitals, virtual_orbitals, occupied_gaps, virtual_gaps, tile_columns, probe_vectors
):
    count_ta = lax.axis_size("ta")
    panel_rows = occupied_orbitals.shape[0]
    slice_width = probe_vectors.shape[1]
    occ_count = occupied_orbitals.shape[1]
    block_count = panel_rows // BLK
    first_block = lax.axis_index("pa") * block_count
    times_grid, cosine_table = quadrature_grids(NT, F_DEV * count_ta)
    occ_weights = jnp.exp(-times_grid[:, None] * occupied_gaps[None, :])
    virt_weights = jnp.exp(-times_grid[:, None] * virtual_gaps[None, :])
    start_terms = jnp.zeros((NT, NVEC, panel_rows), jnp.float32)
    slice_start = lax.axis_index("ta") * slice_width
    owner_panel = slice_start // panel_rows
    offset_rows = slice_start % panel_rows
    local_part = jnp.concatenate(
        [
            lax.dynamic_slice_in_dim(occupied_orbitals, offset_rows, slice_width, 0),
            lax.dynamic_slice_in_dim(virtual_orbitals, offset_rows, slice_width, 0),
        ],
        axis=1,
    )
    column_part = spread(local_part, "pa", owner_panel)
    column_occ = column_part[:, :occ_count]
    column_virt = column_part[:, occ_count:]
    scaled_occ = (column_occ[None].astype(jnp.float32) * occ_weights[:, None, :]).astype(
        jnp.bfloat16
    )
    scaled_virt = (column_virt[None].astype(jnp.float32) * virt_weights[:, None, :]).astype(
        jnp.bfloat16
    )
    panel_tiles = lax.dynamic_slice_in_dim(tile_columns, first_block, block_count, 0)
    column_blocks = (slice_start + jnp.arange(slice_width, dtype=jnp.int32)) // BLK
    present = jnp.any(panel_tiles[:, :, None] == column_blocks[None, None, :], axis=1)
    column_mask = present.astype(jnp.float32)
    empty_terms = jnp.zeros((NT, NVEC, BLK), jnp.float32)

    def block_result(which_block):
        row_occ = lax.dynamic_slice_in_dim(occupied_orbitals, which_block * BLK, BLK, 0)
        row_virt = lax.dynamic_slice_in_dim(virtual_orbitals, which_block * BLK, BLK, 0)
        green_occ = jnp.einsum(
            "tci,ri->tcr", scaled_occ, row_occ, preferred_element_type=jnp.float32
        )
        green_virt = jnp.einsum(
            "tca,ra->tcr", scaled_virt, row_virt, preferred_element_type=jnp.float32
        )
        mask_row = column_mask[which_block]
        polar = (green_occ * green_virt * mask_row[None, :, None]).astype(jnp.bfloat16)
        return jnp.einsum("vc,tcr->tvr", probe_vectors, polar, preferred_element_type=jnp.float32)

    def visit_block(time_terms, which_block):
        block_terms = lax.cond(
            jnp.any(present[which_block]),
            block_result,
            lambda skipped_block: empty_terms,
            which_block,
        )
        return (
            lax.dynamic_update_slice_in_dim(time_terms, block_terms, which_block * BLK, 2),
            None,
        )

    time_terms, _ = lax.scan(visit_block, start_terms, jnp.arange(block_count, dtype=jnp.int32))
    highest = lax.Precision.HIGHEST
    partial_response = jnp.einsum("kt,tvr->kvr", cosine_table, time_terms, precision=highest)
    response = lax.psum_scatter(partial_response, "ta", scatter_dimension=0, tiled=True)
    return response


def solution(mesh):
    placed = (P("pa", None), P("pa", None), P(), P(), P(), P(None, "ta"))
    return jax.shard_map(
        shards, mesh=mesh, in_specs=placed, out_specs=P("ta", None, "pa"), check_vma=False
    )
```

profile of v0, /device:TPU:8, one launch (start us, length us, event | category | flops | bytes accessed | tf_op | source)
XLA Modules:
  0.0 357.0 jit_solution(4372442676124110581)
XLA Ops:
  6.5 1.0 constant_dynamic-slice_fusion.1
  7.5 0.9 constant_dynamic-slice_fusion.2
  10.6 1.5 multiply_exponential_fusion
  13.2 1.4 multiply_exponential_fusion.1
  14.6 77.7 %all-reduce.3.cloned.1.call-done = bf16[64,2048]{1,0:T(8,128)(2,1)} async-done(((bf16[64,2048]{1,0:T(8,128)(2,1)}), bf16[64,2048]{1,0:T(8,128)(2,1)}) %all-reduce.3.cloned.1.call-update) | async-done | bytes 262160 | tf_op jit(solution)/shard_map/psum | solution.py:14
  92.3 1.0 slice_convert_fusion
  93.3 1.5 slice_convert_fusion.1
  95.3 1.6 broadcast_in_dim.7.clone
  96.9 56.1 %while.11 = (s32[]{:T(128)}, f32[32,32,512]{2,0,1:T(8,128)}, s32[4]{0:T(128)}, pred[4,64]{1,0:T(4,128)(4,1)}, bf16[512,512]{1,0:T(8,128)(2,1)}, /*index=5*/bf16[...) while((s32[]{:T(128)}, f32[32,32,512]{2,0,1:T(8,128)}, ...), condition=%wide.region_6.7_spmd.clone, body=%wide.region_2.6_spmd.clone.sunk | while | flops 1099694208 | bytes 21763300 | solution.py:94
  96.9 1.3 dynamic_slice.49
  100.2 1.3 dynamic-slice_reduce_fusion.2
  102.1 5.4 %multiply_convert_fusion.5 = bf16[32,64,1536]{2,1,0:T(8,128)(2,1)} fusion(f32[32,1536]{1,0:T(8,128)} %get-tuple-element.256, f32[64,1536]{1,0:T(8,128)S(1)} %get-tuple-element.257), kind=kLoop, calls=%fused_computation.19.clone.1 | loop fusion | flops 6291456 | bytes 6881280 | tf_op jit(solution)/shard_map/convert_element_type | solution.py:60
  107.5 1.5 multiply_convert_fusion.4
  109.8 1.1 copy_dynamic-update-slice_fusion.2
  110.9 1.3 dynamic_slice.49
  114.3 1.3 dynamic-slice_reduce_fusion.2
  116.1 5.4 %multiply_convert_fusion.5 = bf16[32,64,1536]{2,1,0:T(8,128)(2,1)} fusion(f32[32,1536]{1,0:T(8,128)} %get-tuple-element.256, f32[64,1536]{1,0:T(8,128)S(1)} %get-tuple-element.257), kind=kLoop, calls=%fused_computation.19.clone.1 | loop fusion | flops 6291456 | bytes 6881280 | tf_op jit(solution)/shard_map/convert_element_type | solution.py:60
  121.5 1.5 multiply_convert_fusion.4
  123.8 1.1 copy_dynamic-update-slice_fusion.2
  125.0 1.3 dynamic_slice.49
  128.3 1.3 dynamic-slice_reduce_fusion.2
  130.1 5.4 %multiply_convert_fusion.5 = bf16[32,64,1536]{2,1,0:T(8,128)(2,1)} fusion(f32[32,1536]{1,0:T(8,128)} %get-tuple-element.256, f32[64,1536]{1,0:T(8,128)S(1)} %get-tuple-element.257), kind=kLoop, calls=%fused_computation.19.clone.1 | loop fusion | flops 6291456 | bytes 6881280 | tf_op jit(solution)/shard_map/convert_element_type | solution.py:60
  135.5 1.5 multiply_convert_fusion.4
  137.8 1.1 copy_dynamic-update-slice_fusion.2
  139.0 1.3 dynamic_slice.49
  142.3 1.3 dynamic-slice_reduce_fusion.2
  144.2 5.4 %multiply_convert_fusion.5 = bf16[32,64,1536]{2,1,0:T(8,128)(2,1)} fusion(f32[32,1536]{1,0:T(8,128)} %get-tuple-element.256, f32[64,1536]{1,0:T(8,128)S(1)} %get-tuple-element.257), kind=kLoop, calls=%fused_computation.19.clone.1 | loop fusion | flops 6291456 | bytes 6881280 | tf_op jit(solution)/shard_map/convert_element_type | solution.py:60
  149.5 1.5 multiply_convert_fusion.4
  151.9 1.2 copy_dynamic-update-slice_fusion.2
  153.0 5.3 %fusion.22 = f32[64,32,512]{2,0,1:T(8,128)S(1)} fusion(f32[32,32,512]{2,0,1:T(8,128)} %get-tuple-element.81, f32[32]{0:T(128)} %get-tuple-element.137, f32[64]{0:T(128)} %add_exponential_fusion, f32[32]{0:T(128)} %get-tuple-element.138), kind=kOutput, calls=%fused_computation.28 | convolution fusion | flops 402657280 | bytes 6291968 | tf_op jit(solution)/shard_map/kt,tvr->kvr/dot_general | solution.py:96
  158.4 4.4 %copy.15 = f32[64,32,512]{2,1,0:T(8,128)} copy(f32[64,32,512]{2,0,1:T(8,128)S(1)} %fusion.22) | data formatting | bytes 8388608 | tf_op jit(solution)/shard_map/kt,tvr->kvr/dot_general | solution.py:96
  162.8 187.4 %reduce-scatter.4.cloned.1.call-done = f32[1,32,512]{2,1,0:T(8,128)} async-done(((f32[64,32,512]{2,1,0:T(8,128)}), f32[1,32,512]{2,1,0:T(8,128)}) %reduce-scatter.4.cloned.1.call-update) | async-done | bytes 65552
  (26 shorter events, 4.4 us)
Async XLA Ops:
  6.5 3.3 copy-start
  6.5 85.8 %all-reduce.3.cloned.1.call-start = ((), (), s32[]{:S(2)}) async-start(), calls=%async_computation.1 | async-start | bytes 524288 | tf_op jit(solution)/shard_map/psum | solution.py:14
  7.5 89.4 %copy-start.1 = (bf16[32,64]{1,0:T(8,128)(2,1)S(1)}, bf16[32,64]{1,0:T(8,128)(2,1)}, u32[]{:S(2)}) copy-start(bf16[32,64]{1,0:T(8,128)(2,1)} %param.15) | copy-start | bytes 12292
  9.1 341.1 %reduce-scatter.4.cloned.1.call-start = ((), (), s32[]{:S(2)}) async-start(), calls=%async_computation.2 | async-start | bytes 4259840
Sparse Core Ops, SparseCore 0:
  9.6 82.6 all-reduce.2
  162.9 187.2 reduce-scatter.3
where the time goes:
time: 358 us; the launch traced here: 357 us
  waiting for transfers between devices  265 us (74%)
  other arithmetic  41.2 us (12%)
  local copies, waits for them, and re-layouts  18.3 us (5%)
  loops' own time  13.6 us (4%)
  between operations  13.4 us (4%)
  matrix products  5.32 us (1%)
    unnamed x3, waiting for transfers between devices  187 us
    psum x1, waiting for transfers between devices, spread(): return lax.psum(kept, axis)  77.7 us
    convert_element_type x4, other arithmetic, shards(): (column_virt[None].astype(jnp.float32) * virt_weights[:, None, :]).astype...  21.5 us
    another operation x1, loops' own time, shards(): lax.scan(visit_block, start_terms, jnp.arange(block_count, dtype=jnp.int32))  13.5 us
  transfers between devices with their start and end apart: 2, of which 2 were waited for; matrix products, arithmetic and copies ran while one was open for 2% of the time, Pallas kernels for 0%

commit v1 on v0

--- a/solution.py
+++ b/solution.py
@@ -9,9 +9,15 @@
 F_DEV = 1
 
 
+def summed_here(shard, axis):
+    terms = lax.all_gather(shard, axis, axis=0, tiled=False)
+    summed = terms.sum(axis=0)
+    return summed
+
+
 def spread(value, axis, source):
     kept = jnp.where(lax.axis_index(axis) == source, value, 0).astype(value.dtype)
-    return lax.psum(kept, axis)
+    return summed_here(kept, axis)
 
 
 def quadrature_grids(count_times, count_freqs):

time: 358 us -> 323 us (0.902)
  waiting for transfers between devices: 265 us -> 230 us
    psum x1 -> x0, waiting for transfers between devices: 77.7 us -> none  [spread(): return lax.psum(kept, axis)]
    all_gather x0 -> x1, waiting for transfers between devices: none -> 42.6 us  [summed_here(): terms = lax.all_gather(shard, axis, axis=0, tiled=False)]
where the time goes in v1:
time: 323 us; the launch traced here: 322 us
  waiting for transfers between devices  230 us (71%)
  other arithmetic  41.4 us (13%)
  local copies, waits for them, and re-layouts  18.3 us (6%)
  loops' own time  13.6 us (4%)
  between operations  13.4 us (4%)
  matrix products  5.32 us (2%)
    unnamed x3, waiting for transfers between devices  188 us
    all_gather x1, waiting for transfers between devices, summed_here(): terms = lax.all_gather(shard, axis, axis=0, tiled=False)  42.6 us
    convert_element_type x4, other arithmetic, shards(): (column_virt[None].astype(jnp.float32) * virt_weights[:, None, :]).astype...  21.5 us
    another operation x1, loops' own time, shards(): lax.scan(visit_block, start_terms, jnp.arange(block_count, dtype=jnp.int32))  13.5 us
  transfers between devices with their start and end apart: 2, of which 2 were waited for; matrix products, arithmetic and copies ran while one was open for 2% of the time, Pallas kernels for 0%

profile of v1, /device:TPU:8, one launch (start us, length us, event | category | flops | bytes accessed | tf_op | source)
XLA Modules:
  0.0 322.2 jit_solution(6897014219140031709)
XLA Ops:
  6.5 1.0 dynamic-slice_bitcast_fusion
  7.5 0.9 dynamic-slice_bitcast_fusion.1
  8.3 0.8 maximum_select_fusion
  11.8 1.4 multiply_exponential_fusion.1
  13.2 1.5 multiply_exponential_fusion
  14.6 42.6 %all-gather.2.cloned.1.call-done = bf16[8,64,2048]{2,1,0:T(8,128)(2,1)} async-done(((bf16[1,64,2048]{2,1,0:T(8,128)(2,1)}), bf16[8,64,2048]{2,1,0:T(8,128)(2,1)}) %all-gather.2.cloned.1.call-update) | async-done | bytes 2097168 | tf_op jit(solution)/shard_map/all_gather | solution.py:13
  57.2 2.0 reduce_sum.12
  60.4 1.6 broadcast_in_dim.7.clone
  62.0 56.1 %while.11 = (s32[]{:T(128)}, f32[32,32,512]{2,0,1:T(8,128)}, s32[4]{0:T(128)}, pred[4,64]{1,0:T(4,128)(4,1)}, bf16[512,512]{1,0:T(8,128)(2,1)}, /*index=5*/bf16[...) while((s32[]{:T(128)}, f32[32,32,512]{2,0,1:T(8,128)}, ...), condition=%wide.region_6.7_spmd.clone, body=%wide.region_2.6_spmd.clone.sunk | while | flops 1099694208 | bytes 21763300 | solution.py:100
  62.0 1.3 dynamic_slice.49
  65.3 1.3 dynamic-slice_reduce_fusion.2
  67.2 5.4 %multiply_convert_fusion.5 = bf16[32,64,1536]{2,1,0:T(8,128)(2,1)} fusion(f32[32,1536]{1,0:T(8,128)} %get-tuple-element.256, f32[64,1536]{1,0:T(8,128)S(1)} %get-tuple-element.257), kind=kLoop, calls=%fused_computation.19.clone.1 | loop fusion | flops 6291456 | bytes 6881280 | tf_op jit(solution)/shard_map/convert_element_type | solution.py:66
  72.5 1.5 multiply_convert_fusion.4
  74.9 1.1 copy_dynamic-update-slice_fusion.2
  76.0 1.3 dynamic_slice.49
  79.4 1.3 dynamic-slice_reduce_fusion.2
  81.2 5.4 %multiply_convert_fusion.5 = bf16[32,64,1536]{2,1,0:T(8,128)(2,1)} fusion(f32[32,1536]{1,0:T(8,128)} %get-tuple-element.256, f32[64,1536]{1,0:T(8,128)S(1)} %get-tuple-element.257), kind=kLoop, calls=%fused_computation.19.clone.1 | loop fusion | flops 6291456 | bytes 6881280 | tf_op jit(solution)/shard_map/convert_element_type | solution.py:66
  86.6 1.5 multiply_convert_fusion.4
  88.9 1.1 copy_dynamic-update-slice_fusion.2
  90.1 1.3 dynamic_slice.49
  93.4 1.3 dynamic-slice_reduce_fusion.2
  95.2 5.4 %multiply_convert_fusion.5 = bf16[32,64,1536]{2,1,0:T(8,128)(2,1)} fusion(f32[32,1536]{1,0:T(8,128)} %get-tuple-element.256, f32[64,1536]{1,0:T(8,128)S(1)} %get-tuple-element.257), kind=kLoop, calls=%fused_computation.19.clone.1 | loop fusion | flops 6291456 | bytes 6881280 | tf_op jit(solution)/shard_map/convert_element_type | solution.py:66
  100.6 1.5 multiply_convert_fusion.4
  102.9 1.1 copy_dynamic-update-slice_fusion.2
  104.1 1.3 dynamic_slice.49
  107.4 1.3 dynamic-slice_reduce_fusion.2
  109.2 5.4 %multiply_convert_fusion.5 = bf16[32,64,1536]{2,1,0:T(8,128)(2,1)} fusion(f32[32,1536]{1,0:T(8,128)} %get-tuple-element.256, f32[64,1536]{1,0:T(8,128)S(1)} %get-tuple-element.257), kind=kLoop, calls=%fused_computation.19.clone.1 | loop fusion | flops 6291456 | bytes 6881280 | tf_op jit(solution)/shard_map/convert_element_type | solution.py:66
  114.6 1.5 multiply_convert_fusion.4
  117.0 1.2 copy_dynamic-update-slice_fusion.2
  118.1 5.3 %fusion.22 = f32[64,32,512]{2,0,1:T(8,128)S(1)} fusion(f32[32,32,512]{2,0,1:T(8,128)} %get-tuple-element.81, f32[32]{0:T(128)} %get-tuple-element.137, f32[64]{0:T(128)} %add_exponential_fusion, f32[32]{0:T(128)} %get-tuple-element.138), kind=kOutput, calls=%fused_computation.30 | convolution fusion | flops 402657280 | bytes 6291968 | tf_op jit(solution)/shard_map/kt,tvr->kvr/dot_general | solution.py:102
  123.5 4.4 %copy.15 = f32[64,32,512]{2,1,0:T(8,128)} copy(f32[64,32,512]{2,0,1:T(8,128)S(1)} %fusion.22) | data formatting | bytes 8388608 | tf_op jit(solution)/shard_map/kt,tvr->kvr/dot_general | solution.py:102
  127.8 187.5 %reduce-scatter.4.cloned.1.call-done = f32[1,32,512]{2,1,0:T(8,128)} async-done(((f32[64,32,512]{2,1,0:T(8,128)}), f32[1,32,512]{2,1,0:T(8,128)}) %reduce-scatter.4.cloned.1.call-update) | async-done | bytes 65552
  (27 shorter events, 4.3 us)
Async XLA Ops:
  6.5 2.7 copy-start
  6.5 50.7 %all-gather.2.cloned.1.call-start = ((), (), s32[]{:S(2)}) async-start(), calls=%async_computation.1 | async-start | bytes 2359296 | tf_op jit(solution)/shard_map/all_gather | solution.py:13
  9.2 306.2 %reduce-scatter.4.cloned.1.call-start = ((), (), s32[]{:S(2)}) async-start(), calls=%async_computation.2 | async-start | bytes 4259840
  14.6 47.3 %copy-start.1 = (bf16[32,64]{1,0:T(8,128)(2,1)S(1)}, bf16[32,64]{1,0:T(8,128)(2,1)}, u32[]{:S(2)}) copy-start(bf16[32,64]{1,0:T(8,128)(2,1)} %param.15) | copy-start | bytes 12292
Sparse Core Ops, SparseCore 0:
  9.4 47.7 all-gather.1
  128.0 187.3 reduce-scatter.3
